TPU v7x, 256 devices: a whole 4x4x8 slice. The times are simulated.
256 devices in a mesh: aper: 64 (over z_hi, y, x), shot: 4 (over z_lo, core).
Axes of the slice: x: 4, y: 4, z: 8 (z_hi: 4, z_lo: 2; z = z_hi * 2 + z_lo), core: 2. Of those that a mesh axis runs over, the one named last changes fastest.
Arguments:
- wavefield: float32 [4, 9, 256, 128, 128], P('shot', None, 'aper'), may hold values from -6 to 6
- lame_lambda: float32 [256, 128, 128], P('aper', 'shot'), may hold values from 0.5 to 2
- lame_mu: float32 [256, 128, 128], P('aper', 'shot'), may hold values from 0.3 to 1
- buoyancy: float32 [256, 128, 128], P('aper', 'shot'), may hold values from 0.4 to 1
- quality: float32 [256, 128, 128], P('aper', 'shot'), may hold values from 0.05 to 2
- active: int32 [4, 64, 4, 4], replicated, may hold values 0 or 1
Outputs:
- final_field: float32 [4, 9, 256, 128, 128], P('shot', None, 'aper')
All inputs are finite; a program needn't handle non-finite values.
Results may differ from a plain program's by a relative error of at most 0.00002.
Values sent between devices are 32-bit elements; how exact they have to be, the bound alone decides.
A program may use at most 64 MiB of HBM per device.

v0:
```python
import jax
import jax.numpy as jnp
from jax import lax
from jax.sharding import PartitionSpec as P

BLK = 32
STEPS = 4
COEF_NEAR = 1.125
COEF_FAR = -1.0 / 24.0
TIME_STEP = 0.2


def extended(shard, sides, width):
    for axis, dim in sides:
        devices, length = (lax.axis_size(axis), shard.shape[dim])
        up = [(i, (i + 1) % devices) for i in range(devices - 1)]
        down = [(j, i) for i, j in up]
        last = lax.slice_in_dim(shard, length - width, length, axis=dim)
        initial = lax.slice_in_dim(shard, 0, width, axis=dim)
        before = lax.ppermute(last, axis, up)
        after = lax.ppermute(initial, axis, down)
        shard = jnp.concatenate([before, shard, after], axis=dim)
    return shard


def forward_rows(values, offset, length):
    return COEF_NEAR * (
        values[offset + 1 : offset + 1 + length] - values[offset : offset + length]
    ) + COEF_FAR * (
        values[offset + 2 : offset + 2 + length] - values[offset - 1 : offset - 1 + length]
    )


def backward_rows(values, offset, length):
    return COEF_NEAR * (
        values[offset : offset + length] - values[offset - 1 : offset - 1 + length]
    ) + COEF_FAR * (
        values[offset + 1 : offset + 1 + length] - values[offset - 2 : offset - 2 + length]
    )


def shifted(values, along, amount):
    widths = [(0, 0)] * values.ndim
    widths[along] = (2, 2)
    padded = jnp.pad(values, widths)
    return lax.slice_in_dim(padded, 2 + amount, 2 + amount + values.shape[along], axis=along)


def forward_axis(values, along):
    return COEF_NEAR * (shifted(values, along, 1) - values) + COEF_FAR * (
        shifted(values, along, 2) - shifted(values, along, -1)
    )


def backward_axis(values, along):
    return COEF_NEAR * (values - shifted(values, along, -1)) + COEF_FAR * (
        shifted(values, along, 1) - shifted(values, along, -2)
    )


def velocity_update(previous, stress, offset, length, buoyancy, damping, active_cells):

    def pick_rows(values):
        return values[offset : offset + length]

    grad_first = (
        forward_rows(stress[0], offset, length)
        + backward_axis(pick_rows(stress[3]), 1)
        + backward_axis(pick_rows(stress[4]), 2)
    )
    grad_second = (
        backward_rows(stress[3], offset, length)
        + forward_axis(pick_rows(stress[1]), 1)
        + backward_axis(pick_rows(stress[5]), 2)
    )
    grad_third = (
        backward_rows(stress[4], offset, length)
        + backward_axis(pick_rows(stress[5]), 1)
        + forward_axis(pick_rows(stress[2]), 2)
    )
    forcing = jnp.stack([grad_first, grad_second, grad_third])
    return previous + active_cells * (
        damping * (previous + TIME_STEP * buoyancy * forcing) - previous
    )


def stress_update(previous, velocity, offset, length, lambda_field, shear, damping, active_cells):

    def pick_rows(values):
        return values[offset : offset + length]

    strain_first = backward_rows(velocity[0], offset, length)
    strain_second = backward_axis(pick_rows(velocity[1]), 1)
    strain_third = backward_axis(pick_rows(velocity[2]), 2)
    dilation = strain_first + strain_second + strain_third
    shear_xy = forward_axis(pick_rows(velocity[0]), 1) + forward_rows(velocity[1], offset, length)
    shear_xz = forward_axis(pick_rows(velocity[0]), 2) + forward_rows(velocity[2], offset, length)
    shear_yz = forward_axis(pick_rows(velocity[1]), 2) + forward_axis(pick_rows(velocity[2]), 1)
    rates = jnp.stack(
        [
            lambda_field * dilation + 2.0 * shear * strain_first,
            lambda_field * dilation + 2.0 * shear * strain_second,
            lambda_field * dilation + 2.0 * shear * strain_third,
            shear * shear_xy,
            shear * shear_xz,
            shear * shear_yz,
        ]
    )
    return previous + active_cells * (damping * (previous + TIME_STEP * rates) - previous)


def upsample(blocks):
    return jnp.repeat(jnp.repeat(blocks, BLK, axis=1), BLK, axis=2)


def per_device(wavefield, lame_lambda, lame_mu, buoyancy, quality, active):
    panels = (
        lax.all_gather(lame_lambda, "shot", axis=1, tiled=True),
        lax.all_gather(lame_mu, "shot", axis=1, tiled=True),
        lax.all_gather(buoyancy, "shot", axis=1, tiled=True),
        lax.all_gather(quality, "shot", axis=1, tiled=True),
    )
    model = jnp.stack(panels)
    values = wavefield[0]
    slab_rows = values.shape[1]
    device = lax.axis_index("aper")
    damping = jnp.exp(-TIME_STEP * model[3])
    for moment in range(STEPS):
        blocks = lax.dynamic_index_in_dim(
            active[moment].astype(jnp.float32), device, 0, keepdims=True
        )
        active_cells = upsample(blocks)
        stress_pad = extended(values[3:], (("aper", 1),), 2)
        velocity = velocity_update(
            values[:3], stress_pad, 2, slab_rows, model[2], damping, active_cells
        )
        velocity_pad = extended(velocity, (("aper", 1),), 2)
        stress = stress_update(
            values[3:], velocity_pad, 2, slab_rows, model[0], model[1], damping, active_cells
        )
        values = jnp.concatenate([velocity, stress], axis=0)
    return values[None]


def solution(mesh):
    return jax.shard_map(
        per_device,
        mesh=mesh,
        in_specs=(
            P("shot", None, "aper", None, None),
            P("aper", "shot", None),
            P("aper", "shot", None),
            P("aper", "shot", None),
            P("aper", "shot", None),
            P(),
        ),
        out_specs=P("shot", None, "aper", None, None),
        check_vma=False,
    )
```

profile of v0, /device:TPU:126, one launch (start us, length us, event | category | flops | bytes accessed | tf_op | source)
XLA Modules:
  0.0 352.6 jit_solution(15949601193661434074)
XLA Ops:
  0.0 1.5 slice_bitcast_fusion
  1.5 1.2 fusion.436
  2.8 2.7 collective-permute-start
  5.5 9.4 %collective-permute-start.1 = (f32[6,2,128,128]{3,2,1,0:T(8,128)}, f32[6,2,128,128]{3,2,1,0:T(8,128)}, u32[]{:S(2)}, u32[]{:S(2)}) collective-permute-start(f32[6,2,128,128]{3,2,1,0:T(8,128)} %get-tuple-element.48), channel_id=1, source_target_pairs={{0,4},{4,8},{8,12},{12,16},{16,20},{20,24},{24,28},{28,32},{32,36}... | collective-permute-start | bytes 2359304 | tf_op jit(solution)/shard_map/ppermute | solution.py:20
  15.0 0.6 fusion.441
  15.6 35.7 %all_gather.12 = f32[4,128,128]{2,1,0:T(8,128)S(1)} all-gather(f32[4,32,128]{2,1,0:T(8,128)S(1)} %copy-done.41), channel_id=1, replica_groups=mesh['aper'=64,'shot'=4] {'shot'}, dimensions={1}, use_global_device_ids=true | all-gather | bytes 327680 | tf_op jit(solution)/shard_map/all_gather | solution.py:121
  51.4 5.8 %all_gather.13 = f32[4,128,128]{2,1,0:T(8,128)S(1)} all-gather(f32[4,32,128]{2,1,0:T(8,128)S(1)} %copy-done.42), channel_id=1, replica_groups=mesh['aper'=64,'shot'=4] {'shot'}, dimensions={1}, use_global_device_ids=true | all-gather | bytes 327680 | tf_op jit(solution)/shard_map/all_gather | solution.py:120
  57.7 1.6 slice_bitcast_fusion.32
  59.3 0.6 copy-done
  59.9 1.3 fusion.31
  61.2 1.3 fusion.38
  62.5 1.2 fusion.24
  64.0 0.4 copy-done.15
  64.4 1.9 collective-permute-start.2
  66.3 3.9 %collective-permute-start.3 = (f32[3,2,128,128]{3,2,1,0:T(8,128)S(1)}, f32[3,2,128,128]{3,2,1,0:T(8,128)S(1)}, u32[]{:S(2)}, u32[]{:S(2)}) collective-permute-start(f32[3,2,128,128]{3,2,1,0:T(8,128)S(1)} %get-tuple-element.68), channel_id=1, source_target_pairs={{4,0},{8,4},{12,8},{16,12},{20,16},{24,20},{28,24},{32,28},{36,32}... | collective-permute-start | bytes 1179656 | tf_op jit(solution)/shard_map/ppermute | solution.py:21
  70.3 15.9 %all_gather.15 = f32[4,128,128]{2,1,0:T(8,128)S(1)} all-gather(f32[4,32,128]{2,1,0:T(8,128)S(1)} %copy-done.43), channel_id=1, replica_groups=mesh['aper'=64,'shot'=4] {'shot'}, dimensions={1}, use_global_device_ids=true | all-gather | bytes 327680 | tf_op jit(solution)/shard_map/all_gather | solution.py:119
  86.2 5.8 %all_gather.14 = f32[4,128,128]{2,1,0:T(8,128)S(1)} all-gather(f32[4,32,128]{2,1,0:T(8,128)S(1)} %copy-done.44), channel_id=1, replica_groups=mesh['aper'=64,'shot'=4] {'shot'}, dimensions={1}, use_global_device_ids=true | all-gather | bytes 327680 | tf_op jit(solution)/shard_map/all_gather | solution.py:118
  92.4 0.4 copy-done.19
  94.0 1.2 fusion.435
  95.2 1.9 collective-permute-start.4
  97.1 12.7 %collective-permute-start.5 = (f32[6,2,128,128]{3,2,1,0:T(8,128)}, f32[6,2,128,128]{3,2,1,0:T(8,128)}, u32[]{:S(2)}, u32[]{:S(2)}) collective-permute-start(f32[6,2,128,128]{3,2,1,0:T(8,128)} %get-tuple-element.46), channel_id=1, source_target_pairs={{0,4},{4,8},{8,12},{12,16},{16,20},{20,24},{24,28},{28,32},{32,36}... | collective-permute-start | bytes 2359304 | tf_op jit(solution)/shard_map/ppermute | solution.py:20
  110.1 0.6 broadcast_in_dim.61
  110.8 0.9 copy.10
  111.8 30.2 %collective-permute-done.4 = f32[6,2,128,128]{3,2,1,0:T(8,128)S(1)} collective-permute-done((f32[6,2,128,128]{3,2,1,0:T(8,128)}, f32[6,2,128,128]{3,2,1,0:T(8,128)S(1)}, u32[]{:S(2)}, u32[]{:S(2)}) %collective-permute-start.4) | collective-permute-done | bytes 786464 | tf_op jit(solution)/shard_map/ppermute | solution.py:21
  142.0 2.3 collective-permute-done.5
  144.4 1.3 fusion.75
  145.6 1.3 fusion.82
  147.0 1.2 fusion.68
  148.3 1.6 fusion.9
  150.0 10.7 %collective-permute-start.6 = (f32[3,2,128,128]{3,2,1,0:T(8,128)S(1)}, f32[3,2,128,128]{3,2,1,0:T(8,128)S(1)}, u32[]{:S(2)}, u32[]{:S(2)}) collective-permute-start(f32[3,2,128,128]{3,2,1,0:T(8,128)S(1)} %get-tuple-element.62), channel_id=1, source_target_pairs={{0,4},{4,8},{8,12},{12,16},{16,20},{20,24},{24,28},{28,32},{32,36}... | collective-permute-start | bytes 1179656 | tf_op jit(solution)/shard_map/ppermute | solution.py:20
  160.7 1.9 collective-permute-start.7
  162.7 10.9 %collective-permute-done.6 = f32[3,2,128,128]{3,2,1,0:T(8,128)S(1)} collective-permute-done((f32[3,2,128,128]{3,2,1,0:T(8,128)S(1)}, f32[3,2,128,128]{3,2,1,0:T(8,128)S(1)}, u32[]{:S(2)}, u32[]{:S(2)}) %collective-permute-start.6) | collective-permute-done | bytes 393248 | tf_op jit(solution)/shard_map/ppermute | solution.py:20
  173.5 9.0 %collective-permute-done.7 = f32[3,2,128,128]{3,2,1,0:T(8,128)S(1)} collective-permute-done((f32[3,2,128,128]{3,2,1,0:T(8,128)S(1)}, f32[3,2,128,128]{3,2,1,0:T(8,128)S(1)}, u32[]{:S(2)}, u32[]{:S(2)}) %collective-permute-start.7) | collective-permute-done | bytes 393248 | tf_op jit(solution)/shard_map/ppermute | solution.py:21
  183.6 0.4 copy-done.2
  184.4 1.3 fusion.434
  185.7 1.9 collective-permute-start.8
  187.6 10.2 %collective-permute-start.9 = (f32[6,2,128,128]{3,2,1,0:T(8,128)}, f32[6,2,128,128]{3,2,1,0:T(8,128)S(1)}, u32[]{:S(2)}, u32[]{:S(2)}) collective-permute-start(f32[6,2,128,128]{3,2,1,0:T(8,128)} %get-tuple-element.39), channel_id=1, source_target_pairs={{0,4},{4,8},{8,12},{12,16},{16,20},{20,24},{24,28},{28,32},{32,36}... | collective-permute-start | bytes 2359304 | tf_op jit(solution)/shard_map/ppermute | solution.py:20
  197.9 0.7 copy.21
  198.6 0.8 broadcast_in_dim.63
  199.4 0.7 broadcast_in_dim.64
  200.0 1.3 broadcast_in_dim.65
  201.3 1.6 copy.13
  203.0 25.6 %collective-permute-done.8 = f32[6,2,128,128]{3,2,1,0:T(8,128)S(1)} collective-permute-done((f32[6,2,128,128]{3,2,1,0:T(8,128)}, f32[6,2,128,128]{3,2,1,0:T(8,128)S(1)}, u32[]{:S(2)}, u32[]{:S(2)}) %collective-permute-start.8) | collective-permute-done | bytes 786464 | tf_op jit(solution)/shard_map/ppermute | solution.py:21
  228.6 1.3 collective-permute-done.9
  232.1 1.7 fusion.14
  233.9 10.7 %collective-permute-start.10 = (f32[3,2,128,128]{3,2,1,0:T(8,128)S(1)}, f32[3,2,128,128]{3,2,1,0:T(8,128)S(1)}, u32[]{:S(2)}, u32[]{:S(2)}) collective-permute-start(f32[3,2,128,128]{3,2,1,0:T(8,128)S(1)} %get-tuple-element.57), channel_id=1, source_target_pairs={{0,4},{4,8},{8,12},{12,16},{16,20},{20,24},{24,28},{28,32},{32,36}... | collective-permute-start | bytes 1179656 | tf_op jit(solution)/shard_map/ppermute | solution.py:20
  244.6 2.1 collective-permute-start.11
  246.8 8.4 %collective-permute-done.10 = f32[3,2,128,128]{3,2,1,0:T(8,128)S(1)} collective-permute-done((f32[3,2,128,128]{3,2,1,0:T(8,128)S(1)}, f32[3,2,128,128]{3,2,1,0:T(8,128)S(1)}, u32[]{:S(2)}, u32[]{:S(2)}) %collective-permute-start.10) | collective-permute-done | bytes 393248 | tf_op jit(solution)/shard_map/ppermute | solution.py:20
  255.2 16.0 %collective-permute-done.11 = f32[3,2,128,128]{3,2,1,0:T(8,128)S(1)} collective-permute-done((f32[3,2,128,128]{3,2,1,0:T(8,128)S(1)}, f32[3,2,128,128]{3,2,1,0:T(8,128)S(1)}, u32[]{:S(2)}, u32[]{:S(2)}) %collective-permute-start.11) | collective-permute-done | bytes 393248 | tf_op jit(solution)/shard_map/ppermute | solution.py:21
  272.7 1.3 fusion.433
  274.0 1.9 collective-permute-start.12
  275.9 10.2 %collective-permute-start.13 = (f32[6,2,128,128]{3,2,1,0:T(8,128)}, f32[6,2,128,128]{3,2,1,0:T(8,128)S(1)}, u32[]{:S(2)}, u32[]{:S(2)}) collective-permute-start(f32[6,2,128,128]{3,2,1,0:T(8,128)} %get-tuple-element.32), channel_id=1, source_target_pairs={{0,4},{4,8},{8,12},{12,16},{16,20},{20,24},{24,28},{28,32},{32,36}... | collective-permute-start | bytes 2359304 | tf_op jit(solution)/shard_map/ppermute | solution.py:20
  286.2 0.7 copy.22
  286.9 0.7 broadcast_in_dim.67
  287.7 0.6 broadcast_in_dim.69
  288.3 1.6 copy.16
  290.0 25.6 %collective-permute-done.12 = f32[6,2,128,128]{3,2,1,0:T(8,128)S(1)} collective-permute-done((f32[6,2,128,128]{3,2,1,0:T(8,128)}, f32[6,2,128,128]{3,2,1,0:T(8,128)S(1)}, u32[]{:S(2)}, u32[]{:S(2)}) %collective-permute-start.12) | collective-permute-done | bytes 786464 | tf_op jit(solution)/shard_map/ppermute | solution.py:21
  316.8 0.5 copy-done.4
  318.1 1.8 fusion.19
  320.0 10.6 %collective-permute-start.14 = (f32[3,2,128,128]{3,2,1,0:T(8,128)S(1)}, f32[3,2,128,128]{3,2,1,0:T(8,128)S(1)}, u32[]{:S(2)}, u32[]{:S(2)}) collective-permute-start(f32[3,2,128,128]{3,2,1,0:T(8,128)S(1)} %get-tuple-element.52), channel_id=1, source_target_pairs={{0,4},{4,8},{8,12},{12,16},{16,20},{20,24},{24,28},{28,32},{32,36}... | collective-permute-start | bytes 1179656 | tf_op jit(solution)/shard_map/ppermute | solution.py:20
  330.6 1.9 collective-permute-start.15
  332.6 6.5 %collective-permute-done.14 = f32[3,2,128,128]{3,2,1,0:T(8,128)S(1)} collective-permute-done((f32[3,2,128,128]{3,2,1,0:T(8,128)S(1)}, f32[3,2,128,128]{3,2,1,0:T(8,128)S(1)}, u32[]{:S(2)}, u32[]{:S(2)}) %collective-permute-start.14) | collective-permute-done | bytes 393248 | tf_op jit(solution)/shard_map/ppermute | solution.py:20
  339.1 10.4 %collective-permute-done.15 = f32[3,2,128,128]{3,2,1,0:T(8,128)S(1)} collective-permute-done((f32[3,2,128,128]{3,2,1,0:T(8,128)S(1)}, f32[3,2,128,128]{3,2,1,0:T(8,128)S(1)}, u32[]{:S(2)}, u32[]{:S(2)}) %collective-permute-start.15) | collective-permute-done | bytes 393248 | tf_op jit(solution)/shard_map/ppermute | solution.py:21
  351.0 1.6 maximum_bitcast_fusion
  (155 shorter events, 11.7 us)
Async XLA Ops:
  1.5 13.5 %copy-start.45 = (s32[4,64,4,4]{1,3,2,0:T(4,128)S(1)}, s32[4,64,4,4]{1,3,2,0:T(4,128)}, u32[]{:S(2)}) copy-start(s32[4,64,4,4]{1,3,2,0:T(4,128)} %param.11) | copy-start | bytes 49156
  1.5 14.1 %copy-start.41 = (f32[4,32,128]{2,1,0:T(8,128)S(1)}, f32[4,32,128]{2,1,0:T(8,128)}, u32[]{:S(2)}) copy-start(f32[4,32,128]{2,1,0:T(8,128)} %param.10) | copy-start | bytes 196612
  1.5 49.8 %copy-start.42 = (f32[4,32,128]{2,1,0:T(8,128)S(1)}, f32[4,32,128]{2,1,0:T(8,128)}, u32[]{:S(2)}) copy-start(f32[4,32,128]{2,1,0:T(8,128)} %param.9) | copy-start | bytes 196612
  2.8 56.5 %collective-permute-start = (f32[6,2,128,128]{3,2,1,0:T(8,128)}, f32[6,2,128,128]{3,2,1,0:T(8,128)S(1)}, u32[]{:S(2)}, u32[]{:S(2)}) collective-permute-start(f32[6,2,128,128]{3,2,1,0:T(8,128)} %get-tuple-element.47), channel_id=1, source_target_pairs={{4,0},{8,4},{12,8},{16,12},{20,16},{24,20},{28,24},{32,28},{36,32}... | collective-permute-start | bytes 2359304 | tf_op jit(solution)/shard_map/ppermute | solution.py:21
  5.5 53.8 %collective-permute-start.1 = (f32[6,2,128,128]{3,2,1,0:T(8,128)}, f32[6,2,128,128]{3,2,1,0:T(8,128)}, u32[]{:S(2)}, u32[]{:S(2)}) collective-permute-start(f32[6,2,128,128]{3,2,1,0:T(8,128)} %get-tuple-element.48), channel_id=1, source_target_pairs={{0,4},{4,8},{8,12},{12,16},{16,20},{20,24},{24,28},{28,32},{32,36}... | collective-permute-start | bytes 2359304 | tf_op jit(solution)/shard_map/ppermute | solution.py:20
  57.6 90.6 %copy-start.1 = (f32[4,128,128]{2,1,0:T(8,128)}, f32[4,128,128]{2,1,0:T(8,128)S(1)}, u32[]{:S(2)}) copy-start(f32[4,128,128]{2,1,0:T(8,128)S(1)} %multiply_exponential_fusion) | copy-start | bytes 786436
  57.6 2.2 copy-start
  57.7 90.5 %copy-start.5 = (f32[4,128,128]{2,1,0:T(8,128)}, f32[4,128,128]{2,1,0:T(8,128)S(1)}, u32[]{:S(2)}) copy-start(f32[4,128,128]{2,1,0:T(8,128)S(1)} %broadcast_multiply_fusion.1) | copy-start | bytes 786436
  61.2 87.1 %copy-start.8 = (f32[1,4,128,128]{3,2,1,0:T(8,128)}, f32[1,4,128,128]{3,2,1,0:T(8,128)S(1)}, u32[]{:S(2)}) copy-start(f32[1,4,128,128]{3,2,1,0:T(8,128)S(1)} %fusion.31) | copy-start | bytes 786436
  62.5 1.2 copy-start.11
  63.7 0.7 copy-start.15
  63.7 6.5 %copy-start.43 = (f32[4,32,128]{2,1,0:T(8,128)S(1)}, f32[4,32,128]{2,1,0:T(8,128)}, u32[]{:S(2)}) copy-start(f32[4,32,128]{2,1,0:T(8,128)} %param.8) | copy-start | bytes 196612
  63.9 22.3 %copy-start.44 = (f32[4,32,128]{2,1,0:T(8,128)S(1)}, f32[4,32,128]{2,1,0:T(8,128)}, u32[]{:S(2)}) copy-start(f32[4,32,128]{2,1,0:T(8,128)} %param.7) | copy-start | bytes 196612
  64.4 27.7 %collective-permute-start.2 = (f32[3,2,128,128]{3,2,1,0:T(8,128)S(1)}, f32[3,2,128,128]{3,2,1,0:T(8,128)S(1)}, u32[]{:S(2)}, u32[]{:S(2)}) collective-permute-start(f32[3,2,128,128]{3,2,1,0:T(8,128)S(1)} %get-tuple-element.67), channel_id=1, source_target_pairs={{0,4},{4,8},{8,12},{12,16},{16,20},{20,24},{24,28},{28,32},{32,36}... | collective-permute-start | bytes 1179656 | tf_op jit(solution)/shard_map/ppermute | solution.py:20
  66.3 25.8 %collective-permute-start.3 = (f32[3,2,128,128]{3,2,1,0:T(8,128)S(1)}, f32[3,2,128,128]{3,2,1,0:T(8,128)S(1)}, u32[]{:S(2)}, u32[]{:S(2)}) collective-permute-start(f32[3,2,128,128]{3,2,1,0:T(8,128)S(1)} %get-tuple-element.68), channel_id=1, source_target_pairs={{4,0},{8,4},{12,8},{16,12},{20,16},{24,20},{28,24},{32,28},{36,32}... | collective-permute-start | bytes 1179656 | tf_op jit(solution)/shard_map/ppermute | solution.py:21
  92.1 0.7 copy-start.19
  95.2 46.8 %collective-permute-start.4 = (f32[6,2,128,128]{3,2,1,0:T(8,128)}, f32[6,2,128,128]{3,2,1,0:T(8,128)S(1)}, u32[]{:S(2)}, u32[]{:S(2)}) collective-permute-start(f32[6,2,128,128]{3,2,1,0:T(8,128)} %get-tuple-element.45), channel_id=1, source_target_pairs={{4,0},{8,4},{12,8},{16,12},{20,16},{24,20},{28,24},{32,28},{36,32}... | collective-permute-start | bytes 2359304 | tf_op jit(solution)/shard_map/ppermute | solution.py:21
  97.1 47.2 %collective-permute-start.5 = (f32[6,2,128,128]{3,2,1,0:T(8,128)}, f32[6,2,128,128]{3,2,1,0:T(8,128)}, u32[]{:S(2)}, u32[]{:S(2)}) collective-permute-start(f32[6,2,128,128]{3,2,1,0:T(8,128)} %get-tuple-element.46), channel_id=1, source_target_pairs={{0,4},{4,8},{8,12},{12,16},{16,20},{20,24},{24,28},{28,32},{32,36}... | collective-permute-start | bytes 2359304 | tf_op jit(solution)/shard_map/ppermute | solution.py:20
  145.6 2.6 copy-start.23
  147.0 1.3 copy-start.26
  147.0 1.3 copy-start.12
  147.0 1.3 copy-start.16
  148.3 1.6 copy-start.29
  149.9 32.6 %copy-start.20 = (f32[4,128,128]{2,1,0:T(8,128)S(1)}, f32[4,128,128]{2,1,0:T(8,128)}, u32[]{:S(2)}) copy-start(f32[4,128,128]{2,1,0:T(8,128)} %copy-done.19) | copy-start | bytes 786436
  150.0 23.6 %collective-permute-start.6 = (f32[3,2,128,128]{3,2,1,0:T(8,128)S(1)}, f32[3,2,128,128]{3,2,1,0:T(8,128)S(1)}, u32[]{:S(2)}, u32[]{:S(2)}) collective-permute-start(f32[3,2,128,128]{3,2,1,0:T(8,128)S(1)} %get-tuple-element.62), channel_id=1, source_target_pairs={{0,4},{4,8},{8,12},{12,16},{16,20},{20,24},{24,28},{28,32},{32,36}... | collective-permute-start | bytes 1179656 | tf_op jit(solution)/shard_map/ppermute | solution.py:20
  160.7 21.8 %collective-permute-start.7 = (f32[3,2,128,128]{3,2,1,0:T(8,128)S(1)}, f32[3,2,128,128]{3,2,1,0:T(8,128)S(1)}, u32[]{:S(2)}, u32[]{:S(2)}) collective-permute-start(f32[3,2,128,128]{3,2,1,0:T(8,128)S(1)} %get-tuple-element.63), channel_id=1, source_target_pairs={{4,0},{8,4},{12,8},{16,12},{20,16},{24,20},{28,24},{32,28},{36,32}... | collective-permute-start | bytes 1179656 | tf_op jit(solution)/shard_map/ppermute | solution.py:21
  183.1 1.0 copy-start.2
  184.4 13.5 %copy-start.46 = (s32[1,64,4,4]{1,3,2,0:T(4,128)S(1)}, s32[1,64,4,4]{1,3,2,0:T(4,128)}, u32[]{:S(2)}) copy-start(s32[1,64,4,4]{1,3,2,0:T(4,128)} %get-tuple-element.69) | copy-start | bytes 12292
  184.4 13.5 %copy-start.47 = (s32[1,64,4,4]{1,3,2,0:T(4,128)S(1)}, s32[1,64,4,4]{1,3,2,0:T(4,128)}, u32[]{:S(2)}) copy-start(s32[1,64,4,4]{1,3,2,0:T(4,128)} %get-tuple-element.72) | copy-start | bytes 12292
  185.7 43.0 %collective-permute-start.8 = (f32[6,2,128,128]{3,2,1,0:T(8,128)}, f32[6,2,128,128]{3,2,1,0:T(8,128)S(1)}, u32[]{:S(2)}, u32[]{:S(2)}) collective-permute-start(f32[6,2,128,128]{3,2,1,0:T(8,128)} %get-tuple-element.38), channel_id=1, source_target_pairs={{4,0},{8,4},{12,8},{16,12},{20,16},{24,20},{28,24},{32,28},{36,32}... | collective-permute-start | bytes 2359304 | tf_op jit(solution)/shard_map/ppermute | solution.py:21
  187.6 42.3 %collective-permute-start.9 = (f32[6,2,128,128]{3,2,1,0:T(8,128)}, f32[6,2,128,128]{3,2,1,0:T(8,128)S(1)}, u32[]{:S(2)}, u32[]{:S(2)}) collective-permute-start(f32[6,2,128,128]{3,2,1,0:T(8,128)} %get-tuple-element.39), channel_id=1, source_target_pairs={{0,4},{4,8},{8,12},{12,16},{16,20},{20,24},{24,28},{28,32},{32,36}... | collective-permute-start | bytes 2359304 | tf_op jit(solution)/shard_map/ppermute | solution.py:20
  230.2 0.7 copy-start.32
  230.5 0.7 copy-start.34
  230.5 1.0 copy-start.3
  230.5 1.1 copy-start.6
  230.5 1.2 copy-start.9
  230.6 1.3 copy-start.13
  230.6 1.3 copy-start.17
  230.6 1.4 copy-start.24
  230.6 1.5 copy-start.27
  230.6 1.5 copy-start.30
  230.6 1.5 copy-start.38
  232.1 1.7 copy-start.36
  233.8 37.4 %copy-start.21 = (f32[4,128,128]{2,1,0:T(8,128)S(1)}, f32[4,128,128]{2,1,0:T(8,128)}, u32[]{:S(2)}) copy-start(f32[4,128,128]{2,1,0:T(8,128)} %copy-done.19) | copy-start | bytes 786436
  233.9 21.3 %collective-permute-start.10 = (f32[3,2,128,128]{3,2,1,0:T(8,128)S(1)}, f32[3,2,128,128]{3,2,1,0:T(8,128)S(1)}, u32[]{:S(2)}, u32[]{:S(2)}) collective-permute-start(f32[3,2,128,128]{3,2,1,0:T(8,128)S(1)} %get-tuple-element.57), channel_id=1, source_target_pairs={{0,4},{4,8},{8,12},{12,16},{16,20},{20,24},{24,28},{28,32},{32,36}... | collective-permute-start | bytes 1179656 | tf_op jit(solution)/shard_map/ppermute | solution.py:20
  244.6 26.6 %collective-permute-start.11 = (f32[3,2,128,128]{3,2,1,0:T(8,128)S(1)}, f32[3,2,128,128]{3,2,1,0:T(8,128)S(1)}, u32[]{:S(2)}, u32[]{:S(2)}) collective-permute-start(f32[3,2,128,128]{3,2,1,0:T(8,128)S(1)} %get-tuple-element.58), channel_id=1, source_target_pairs={{4,0},{8,4},{12,8},{16,12},{20,16},{24,20},{28,24},{32,28},{36,32}... | collective-permute-start | bytes 1179656 | tf_op jit(solution)/shard_map/ppermute | solution.py:21
  274.0 41.6 %collective-permute-start.12 = (f32[6,2,128,128]{3,2,1,0:T(8,128)}, f32[6,2,128,128]{3,2,1,0:T(8,128)S(1)}, u32[]{:S(2)}, u32[]{:S(2)}) collective-permute-start(f32[6,2,128,128]{3,2,1,0:T(8,128)} %get-tuple-element.31), channel_id=1, source_target_pairs={{4,0},{8,4},{12,8},{16,12},{20,16},{24,20},{28,24},{32,28},{36,32}... | collective-permute-start | bytes 2359304 | tf_op jit(solution)/shard_map/ppermute | solution.py:21
  275.9 39.9 %collective-permute-start.13 = (f32[6,2,128,128]{3,2,1,0:T(8,128)}, f32[6,2,128,128]{3,2,1,0:T(8,128)S(1)}, u32[]{:S(2)}, u32[]{:S(2)}) collective-permute-start(f32[6,2,128,128]{3,2,1,0:T(8,128)} %get-tuple-element.32), channel_id=1, source_target_pairs={{0,4},{4,8},{8,12},{12,16},{16,20},{20,24},{24,28},{28,32},{32,36}... | collective-permute-start | bytes 2359304 | tf_op jit(solution)/shard_map/ppermute | solution.py:20
  316.4 1.0 copy-start.4
  316.4 1.0 copy-start.7
  316.4 1.1 copy-start.10
  316.4 1.2 copy-start.14
  316.4 1.2 copy-start.18
  316.4 1.3 copy-start.25
  316.4 1.4 copy-start.28
  316.4 1.4 copy-start.31
  316.4 1.5 copy-start.33
  316.4 1.6 copy-start.35
  316.5 1.7 copy-start.37
  316.5 1.7 copy-start.39
  316.5 1.6 copy-start.40
  319.9 29.7 %copy-start.22 = (f32[4,128,128]{2,1,0:T(8,128)S(1)}, f32[4,128,128]{2,1,0:T(8,128)}, u32[]{:S(2)}) copy-start(f32[4,128,128]{2,1,0:T(8,128)} %copy-done.19) | copy-start | bytes 786436
  320.0 19.2 %collective-permute-start.14 = (f32[3,2,128,128]{3,2,1,0:T(8,128)S(1)}, f32[3,2,128,128]{3,2,1,0:T(8,128)S(1)}, u32[]{:S(2)}, u32[]{:S(2)}) collective-permute-start(f32[3,2,128,128]{3,2,1,0:T(8,128)S(1)} %get-tuple-element.52), channel_id=1, source_target_pairs={{0,4},{4,8},{8,12},{12,16},{16,20},{20,24},{24,28},{28,32},{32,36}... | collective-permute-start | bytes 1179656 | tf_op jit(solution)/shard_map/ppermute | solution.py:20
  330.6 19.0 %collective-permute-start.15 = (f32[3,2,128,128]{3,2,1,0:T(8,128)S(1)}, f32[3,2,128,128]{3,2,1,0:T(8,128)S(1)}, u32[]{:S(2)}, u32[]{:S(2)}) collective-permute-start(f32[3,2,128,128]{3,2,1,0:T(8,128)S(1)} %get-tuple-element.53), channel_id=1, source_target_pairs={{4,0},{8,4},{12,8},{16,12},{20,16},{24,20},{28,24},{32,28},{36,32}... | collective-permute-start | bytes 1179656 | tf_op jit(solution)/shard_map/ppermute | solution.py:21
where the time goes:
time: 354 us; the launch traced here: 353 us
  waiting for transfers between devices  146 us (41%)
  starting transfers between devices  94.9 us (27%)
  blocking collectives  63.3 us (18%)
  local copies, waits for them, and re-layouts  24.8 us (7%)
  other arithmetic  22.2 us (6%)
    ppermute x8, waiting for transfers between devices, extended(): after = lax.ppermute(initial, axis, down)  117 us
    ppermute x8, starting transfers between devices, extended(): before = lax.ppermute(last, axis, up)  76.6 us
    all_gather x1, blocking collectives, per_device(): lax.all_gather(quality, 'shot', axis=1, tiled=True)  35.7 us
    ppermute x8, waiting for transfers between devices, extended(): before = lax.ppermute(last, axis, up)  29.6 us
    ppermute x8, starting transfers between devices, extended(): after = lax.ppermute(initial, axis, down)  18.3 us
    all_gather x1, blocking collectives, per_device(): lax.all_gather(lame_mu, 'shot', axis=1, tiled=True)  15.9 us
    another operation x12, other arithmetic, velocity_update(): forcing = jnp.stack([grad_first, grad_second, grad_third])  9.36 us
    broadcast_in_dim x16, local copies, waits for them, and re-layouts, upsample(): return jnp.repeat(jnp.repeat(blocks, BLK, axis=1), BLK, axis=2)  9.27 us
  transfers between devices with their start and end apart: 16, of which 12 were waited for; matrix products, arithmetic and copies ran while one was open for 4% of the time, Pallas kernels for 0%

commit v1 on v0

--- a/solution.py
+++ b/solution.py
@@ -118,7 +118,9 @@
         lax.all_gather(lame_lambda, "shot", axis=1, tiled=True),
         lax.all_gather(lame_mu, "shot", axis=1, tiled=True),
         lax.all_gather(buoyancy, "shot", axis=1, tiled=True),
-        lax.all_gather(quality, "shot", axis=1, tiled=True),
+        jnp.concatenate(
+            lax.all_to_all(jnp.stack([quality] * lax.axis_size("shot")), "shot", 0, 0), axis=1
+        ),
     )
     model = jnp.stack(panels)
     values = wavefield[0]

time: 354 us -> 338 us (0.955); the launches traced: 353 us -> 333 us
  blocking collectives: 63.3 us -> 52.3 us
  waiting for transfers between devices: 146 us -> 137 us
    all_gather x1 -> x0, blocking collectives: 35.7 us -> none  [per_device(): lax.all_gather(quality, 'shot', axis=1, tiled=True)]
    all_gather x1, blocking collectives: 5.84 us -> 34 us  [per_device(): lax.all_gather(buoyancy, 'shot', axis=1, tiled=True)]
    ppermute x8, waiting for transfers between devices: 117 us -> 99.6 us  [extended(): after = lax.ppermute(initial, axis, down)]
    ppermute x8, waiting for transfers between devices: 29.6 us -> 37.3 us  [extended(): before = lax.ppermute(last, axis, up)]
    all_to_all x0 -> x1, starting transfers between devices: none -> 4.1 us  [per_device(): lax.all_to_all(jnp.stack([quality] * lax.axis_size('shot')), 'shot', 0, 0)]
    another operation x12, other arithmetic: 9.36 us -> 5.43 us  [velocity_update(): forcing = jnp.stack([grad_first, grad_second, grad_third])]
    ppermute x8, starting transfers between devices: 76.6 us -> 72.7 us  [extended(): before = lax.ppermute(last, axis, up)]
  transfers between devices with their start and end apart: 16 -> 17, of which waited for: 12 -> 11; matrix products, arithmetic and copies ran while one was open for 4% -> 5% of each run, Pallas kernels for 0% -> 0%
where the time goes in v1:
time: 338 us; the launch traced here: 333 us
  waiting for transfers between devices  137 us (41%)
  starting transfers between devices  95.1 us (28%)
  blocking collectives  52.3 us (15%)
  local copies, waits for them, and re-layouts  27.4 us (8%)
  other arithmetic  20.1 us (6%)
    ppermute x8, waiting for transfers between devices, extended(): after = lax.ppermute(initial, axis, down)  99.6 us
    ppermute x8, starting transfers between devices, extended(): before = lax.ppermute(last, axis, up)  72.7 us
    ppermute x8, waiting for transfers between devices, extended(): before = lax.ppermute(last, axis, up)  37.3 us
    all_gather x1, blocking collectives, per_device(): lax.all_gather(buoyancy, 'shot', axis=1, tiled=True)  34 us
    ppermute x8, starting transfers between devices, extended(): after = lax.ppermute(initial, axis, down)  18.3 us
    all_gather x1, blocking collectives, per_device(): lax.all_gather(lame_mu, 'shot', axis=1, tiled=True)  12.4 us
    broadcast_in_dim x16, local copies, waits for them, and re-layouts, upsample(): return jnp.repeat(jnp.repeat(blocks, BLK, axis=1), BLK, axis=2)  9.32 us
  transfers between devices with their start and end apart: 17, of which 11 were waited for; matrix products, arithmetic and copies ran while one was open for 5% of the time, Pallas kernels for 0%

profile of v1, /device:TPU:126, one launch (start us, length us, event | category | flops | bytes accessed | tf_op | source)
XLA Modules:
  0.0 332.9 jit_solution(10323474194153710229)
XLA Ops:
  0.0 1.5 slice_bitcast_fusion
  1.5 1.2 fusion.437
  2.8 2.7 collective-permute-start
  5.5 9.4 %collective-permute-start.1 = (f32[6,2,128,128]{3,2,1,0:T(8,128)}, f32[6,2,128,128]{3,2,1,0:T(8,128)S(1)}, u32[]{:S(2)}, u32[]{:S(2)}) collective-permute-start(f32[6,2,128,128]{3,2,1,0:T(8,128)} %get-tuple-element.48), channel_id=1, source_target_pairs={{0,4},{4,8},{8,12},{12,16},{16,20},{20,24},{24,28},{28,32},{32,36}... | collective-permute-start | bytes 2359304 | tf_op jit(solution)/shard_map/ppermute | solution.py:20
  15.0 0.7 stack.139
  15.7 4.1 %all-to-all-start = ((f32[4,4,32,128]{3,2,1,0:T(8,128)}), f32[4,4,32,128]{3,2,1,0:T(8,128)}, u32[]{:S(2)}, u32[]{:S(2)}) async-start(f32[4,4,32,128]{3,2,1,0:T(8,128)} %stack.139), calls=%async_computation | async-start | bytes 524288 | tf_op jit(solution)/shard_map/all_to_all | solution.py:122
  19.8 0.6 fusion.442
  20.5 34.0 %all_gather.9 = f32[4,128,128]{2,1,0:T(8,128)} all-gather(f32[4,32,128]{2,1,0:T(8,128)S(1)} %copy-done.48), channel_id=1, replica_groups=mesh['aper'=64,'shot'=4] {'shot'}, dimensions={1}, use_global_device_ids=true | all-gather | bytes 327680 | tf_op jit(solution)/shard_map/all_gather | solution.py:120
  54.9 1.0 broadcast_multiply_fusion.1
  55.9 2.5 slice_bitcast_fusion.32
  58.4 1.0 fusion.381
  59.4 2.2 fusion.31
  62.2 0.6 copy-done.43
  63.6 0.4 copy-done.17
  64.0 1.9 collective-permute-start.2
  65.9 3.9 %collective-permute-start.3 = (f32[3,2,128,128]{3,2,1,0:T(8,128)S(1)}, f32[3,2,128,128]{3,2,1,0:T(8,128)S(1)}, u32[]{:S(2)}, u32[]{:S(2)}) collective-permute-start(f32[3,2,128,128]{3,2,1,0:T(8,128)S(1)} %get-tuple-element.68), channel_id=1, source_target_pairs={{4,0},{8,4},{12,8},{16,12},{20,16},{24,20},{28,24},{32,28},{36,32}... | collective-permute-start | bytes 1179656 | tf_op jit(solution)/shard_map/ppermute | solution.py:21
  69.8 12.4 %all_gather.11 = f32[4,128,128]{2,1,0:T(8,128)S(1)} all-gather(f32[4,32,128]{2,1,0:T(8,128)S(1)} %copy-done.49), channel_id=1, replica_groups=mesh['aper'=64,'shot'=4] {'shot'}, dimensions={1}, use_global_device_ids=true | all-gather | bytes 327680 | tf_op jit(solution)/shard_map/all_gather | solution.py:119
  82.3 5.8 %all_gather.10 = f32[4,128,128]{2,1,0:T(8,128)S(1)} all-gather(f32[4,32,128]{2,1,0:T(8,128)S(1)} %copy-done.50), channel_id=1, replica_groups=mesh['aper'=64,'shot'=4] {'shot'}, dimensions={1}, use_global_device_ids=true | all-gather | bytes 327680 | tf_op jit(solution)/shard_map/all_gather | solution.py:118
  90.0 1.2 fusion.436
  91.2 1.9 collective-permute-start.4
  93.2 13.1 %collective-permute-start.5 = (f32[6,2,128,128]{3,2,1,0:T(8,128)}, f32[6,2,128,128]{3,2,1,0:T(8,128)S(1)}, u32[]{:S(2)}, u32[]{:S(2)}) collective-permute-start(f32[6,2,128,128]{3,2,1,0:T(8,128)} %get-tuple-element.46), channel_id=1, source_target_pairs={{0,4},{4,8},{8,12},{12,16},{16,20},{20,24},{24,28},{28,32},{32,36}... | collective-permute-start | bytes 2359304 | tf_op jit(solution)/shard_map/ppermute | solution.py:20
  106.5 0.6 broadcast_in_dim.61
  107.1 0.9 copy.35
  108.2 30.9 %collective-permute-done.4 = f32[6,2,128,128]{3,2,1,0:T(8,128)S(1)} collective-permute-done((f32[6,2,128,128]{3,2,1,0:T(8,128)}, f32[6,2,128,128]{3,2,1,0:T(8,128)S(1)}, u32[]{:S(2)}, u32[]{:S(2)}) %collective-permute-start.4) | collective-permute-done | bytes 786464 | tf_op jit(solution)/shard_map/ppermute | solution.py:21
  139.1 1.6 collective-permute-done.5
  141.7 0.3 copy-done.28
  142.1 0.7 copy-done.31
  142.8 1.5 fusion.9
  144.4 10.7 %collective-permute-start.6 = (f32[3,2,128,128]{3,2,1,0:T(8,128)S(1)}, f32[3,2,128,128]{3,2,1,0:T(8,128)S(1)}, u32[]{:S(2)}, u32[]{:S(2)}) collective-permute-start(f32[3,2,128,128]{3,2,1,0:T(8,128)S(1)} %get-tuple-element.62), channel_id=1, source_target_pairs={{0,4},{4,8},{8,12},{12,16},{16,20},{20,24},{24,28},{28,32},{32,36}... | collective-permute-start | bytes 1179656 | tf_op jit(solution)/shard_map/ppermute | solution.py:20
  155.1 1.9 collective-permute-start.7
  157.1 13.1 %collective-permute-done.6 = f32[3,2,128,128]{3,2,1,0:T(8,128)S(1)} collective-permute-done((f32[3,2,128,128]{3,2,1,0:T(8,128)S(1)}, f32[3,2,128,128]{3,2,1,0:T(8,128)S(1)}, u32[]{:S(2)}, u32[]{:S(2)}) %collective-permute-start.6) | collective-permute-done | bytes 393248 | tf_op jit(solution)/shard_map/ppermute | solution.py:20
  170.2 14.3 %collective-permute-done.7 = f32[3,2,128,128]{3,2,1,0:T(8,128)S(1)} collective-permute-done((f32[3,2,128,128]{3,2,1,0:T(8,128)S(1)}, f32[3,2,128,128]{3,2,1,0:T(8,128)S(1)}, u32[]{:S(2)}, u32[]{:S(2)}) %collective-permute-start.7) | collective-permute-done | bytes 393248 | tf_op jit(solution)/shard_map/ppermute | solution.py:21
  185.7 0.3 multiply_add_fusion.2
  186.1 1.2 fusion.435
  187.3 1.9 collective-permute-start.8
  189.2 10.2 %collective-permute-start.9 = (f32[6,2,128,128]{3,2,1,0:T(8,128)}, f32[6,2,128,128]{3,2,1,0:T(8,128)S(1)}, u32[]{:S(2)}, u32[]{:S(2)}) collective-permute-start(f32[6,2,128,128]{3,2,1,0:T(8,128)} %get-tuple-element.39), channel_id=1, source_target_pairs={{0,4},{4,8},{8,12},{12,16},{16,20},{20,24},{24,28},{28,32},{32,36}... | collective-permute-start | bytes 2359304 | tf_op jit(solution)/shard_map/ppermute | solution.py:20
  199.6 0.7 copy.46
  200.3 0.8 broadcast_in_dim.63
  201.0 0.7 broadcast_in_dim.64
  201.7 1.3 broadcast_in_dim.65
  203.0 1.6 copy.38
  204.7 25.4 %collective-permute-done.8 = f32[6,2,128,128]{3,2,1,0:T(8,128)S(1)} collective-permute-done((f32[6,2,128,128]{3,2,1,0:T(8,128)}, f32[6,2,128,128]{3,2,1,0:T(8,128)S(1)}, u32[]{:S(2)}, u32[]{:S(2)}) %collective-permute-start.8) | collective-permute-done | bytes 786464 | tf_op jit(solution)/shard_map/ppermute | solution.py:21
  232.2 1.7 fusion.14
  234.0 6.5 %collective-permute-start.10 = (f32[3,2,128,128]{3,2,1,0:T(8,128)S(1)}, f32[3,2,128,128]{3,2,1,0:T(8,128)S(1)}, u32[]{:S(2)}, u32[]{:S(2)}) collective-permute-start(f32[3,2,128,128]{3,2,1,0:T(8,128)S(1)} %get-tuple-element.57), channel_id=1, source_target_pairs={{0,4},{4,8},{8,12},{12,16},{16,20},{20,24},{24,28},{28,32},{32,36}... | collective-permute-start | bytes 1179656 | tf_op jit(solution)/shard_map/ppermute | solution.py:20
  240.5 2.1 collective-permute-start.11
  242.7 7.1 %collective-permute-done.10 = f32[3,2,128,128]{3,2,1,0:T(8,128)S(1)} collective-permute-done((f32[3,2,128,128]{3,2,1,0:T(8,128)S(1)}, f32[3,2,128,128]{3,2,1,0:T(8,128)S(1)}, u32[]{:S(2)}, u32[]{:S(2)}) %collective-permute-start.10) | collective-permute-done | bytes 393248 | tf_op jit(solution)/shard_map/ppermute | solution.py:20
  249.7 6.8 %collective-permute-done.11 = f32[3,2,128,128]{3,2,1,0:T(8,128)S(1)} collective-permute-done((f32[3,2,128,128]{3,2,1,0:T(8,128)S(1)}, f32[3,2,128,128]{3,2,1,0:T(8,128)S(1)}, u32[]{:S(2)}, u32[]{:S(2)}) %collective-permute-start.11) | collective-permute-done | bytes 393248 | tf_op jit(solution)/shard_map/ppermute | solution.py:21
  257.7 0.3 multiply_add_fusion.1
  258.0 1.2 fusion.434
  259.3 1.9 collective-permute-start.12
  261.2 10.2 %collective-permute-start.13 = (f32[6,2,128,128]{3,2,1,0:T(8,128)}, f32[6,2,128,128]{3,2,1,0:T(8,128)S(1)}, u32[]{:S(2)}, u32[]{:S(2)}) collective-permute-start(f32[6,2,128,128]{3,2,1,0:T(8,128)} %get-tuple-element.32), channel_id=1, source_target_pairs={{0,4},{4,8},{8,12},{12,16},{16,20},{20,24},{24,28},{28,32},{32,36}... | collective-permute-start | bytes 2359304 | tf_op jit(solution)/shard_map/ppermute | solution.py:20
  271.4 0.7 copy.47
  272.1 0.7 broadcast_in_dim.67
  272.9 0.6 broadcast_in_dim.69
  273.6 1.6 copy.41
  275.3 14.1 %collective-permute-done.12 = f32[6,2,128,128]{3,2,1,0:T(8,128)S(1)} collective-permute-done((f32[6,2,128,128]{3,2,1,0:T(8,128)}, f32[6,2,128,128]{3,2,1,0:T(8,128)S(1)}, u32[]{:S(2)}, u32[]{:S(2)}) %collective-permute-start.12) | collective-permute-done | bytes 786464 | tf_op jit(solution)/shard_map/ppermute | solution.py:21
  289.3 9.6 %collective-permute-done.13 = f32[6,2,128,128]{3,2,1,0:T(8,128)S(1)} collective-permute-done((f32[6,2,128,128]{3,2,1,0:T(8,128)}, f32[6,2,128,128]{3,2,1,0:T(8,128)S(1)}, u32[]{:S(2)}, u32[]{:S(2)}) %collective-permute-start.13) | collective-permute-done | bytes 786464 | tf_op jit(solution)/shard_map/ppermute | solution.py:20
  299.9 0.5 copy-done.4
  301.3 1.8 fusion.19
  303.1 10.6 %collective-permute-start.14 = (f32[3,2,128,128]{3,2,1,0:T(8,128)S(1)}, f32[3,2,128,128]{3,2,1,0:T(8,128)S(1)}, u32[]{:S(2)}, u32[]{:S(2)}) collective-permute-start(f32[3,2,128,128]{3,2,1,0:T(8,128)S(1)} %get-tuple-element.52), channel_id=1, source_target_pairs={{0,4},{4,8},{8,12},{12,16},{16,20},{20,24},{24,28},{28,32},{32,36}... | collective-permute-start | bytes 1179656 | tf_op jit(solution)/shard_map/ppermute | solution.py:20
  313.7 1.9 collective-permute-start.15
  315.7 5.9 %collective-permute-done.14 = f32[3,2,128,128]{3,2,1,0:T(8,128)S(1)} collective-permute-done((f32[3,2,128,128]{3,2,1,0:T(8,128)S(1)}, f32[3,2,128,128]{3,2,1,0:T(8,128)S(1)}, u32[]{:S(2)}, u32[]{:S(2)}) %collective-permute-start.14) | collective-permute-done | bytes 393248 | tf_op jit(solution)/shard_map/ppermute | solution.py:20
  321.6 8.2 %collective-permute-done.15 = f32[3,2,128,128]{3,2,1,0:T(8,128)S(1)} collective-permute-done((f32[3,2,128,128]{3,2,1,0:T(8,128)S(1)}, f32[3,2,128,128]{3,2,1,0:T(8,128)S(1)}, u32[]{:S(2)}, u32[]{:S(2)}) %collective-permute-start.15) | collective-permute-done | bytes 393248 | tf_op jit(solution)/shard_map/ppermute | solution.py:21
  331.3 1.6 maximum_bitcast_fusion
  (169 shorter events, 13.1 us)
Async XLA Ops:
  1.5 13.5 %copy-start.47 = (f32[4,32,128]{2,1,0:T(8,128)S(1)}, f32[4,32,128]{2,1,0:T(8,128)}, u32[]{:S(2)}) copy-start(f32[4,32,128]{2,1,0:T(8,128)} %param.10) | copy-start | bytes 196612
  1.5 18.3 %copy-start.51 = (s32[4,64,4,4]{1,3,2,0:T(4,128)S(1)}, s32[4,64,4,4]{1,3,2,0:T(4,128)}, u32[]{:S(2)}) copy-start(s32[4,64,4,4]{1,3,2,0:T(4,128)} %param.11) | copy-start | bytes 49156
  1.5 19.0 %copy-start.48 = (f32[4,32,128]{2,1,0:T(8,128)S(1)}, f32[4,32,128]{2,1,0:T(8,128)}, u32[]{:S(2)}) copy-start(f32[4,32,128]{2,1,0:T(8,128)} %param.9) | copy-start | bytes 196612
  2.8 56.6 %collective-permute-start = (f32[6,2,128,128]{3,2,1,0:T(8,128)}, f32[6,2,128,128]{3,2,1,0:T(8,128)S(1)}, u32[]{:S(2)}, u32[]{:S(2)}) collective-permute-start(f32[6,2,128,128]{3,2,1,0:T(8,128)} %get-tuple-element.47), channel_id=1, source_target_pairs={{4,0},{8,4},{12,8},{16,12},{20,16},{24,20},{28,24},{32,28},{36,32}... | collective-permute-start | bytes 2359304 | tf_op jit(solution)/shard_map/ppermute | solution.py:21
  5.5 53.9 %collective-permute-start.1 = (f32[6,2,128,128]{3,2,1,0:T(8,128)}, f32[6,2,128,128]{3,2,1,0:T(8,128)S(1)}, u32[]{:S(2)}, u32[]{:S(2)}) collective-permute-start(f32[6,2,128,128]{3,2,1,0:T(8,128)} %get-tuple-element.48), channel_id=1, source_target_pairs={{0,4},{4,8},{8,12},{12,16},{16,20},{20,24},{24,28},{28,32},{32,36}... | collective-permute-start | bytes 2359304 | tf_op jit(solution)/shard_map/ppermute | solution.py:20
  15.7 42.7 %all-to-all-start = ((f32[4,4,32,128]{3,2,1,0:T(8,128)}), f32[4,4,32,128]{3,2,1,0:T(8,128)}, u32[]{:S(2)}, u32[]{:S(2)}) async-start(f32[4,4,32,128]{3,2,1,0:T(8,128)} %stack.139), calls=%async_computation | async-start | bytes 524288 | tf_op jit(solution)/shard_map/all_to_all | solution.py:122
  55.9 7.4 %copy-start.5 = (f32[4,128,128]{2,1,0:T(8,128)}, f32[4,128,128]{2,1,0:T(8,128)S(1)}, u32[]{:S(2)}) copy-start(f32[4,128,128]{2,1,0:T(8,128)S(1)} %broadcast_multiply_fusion.1) | copy-start | bytes 786436
  59.4 30.3 %copy-start.1 = (f32[4,4,32,128]{3,2,0,1:T(8,128)}, f32[4,4,32,128]{3,2,0,1:T(8,128)S(1)}, u32[]{:S(2)}) copy-start(f32[4,4,32,128]{3,2,0,1:T(8,128)S(1)} %fusion.381) | copy-start | bytes 786436
  59.4 2.5 copy-start
  59.4 2.4 copy-start.34
  59.4 2.5 copy-start.45
  61.6 1.6 copy-start.9
  61.9 0.9 copy-start.43
  61.9 1.0 copy-start.44
  62.2 1.1 copy-start.13
  63.3 6.5 %copy-start.49 = (f32[4,32,128]{2,1,0:T(8,128)S(1)}, f32[4,32,128]{2,1,0:T(8,128)}, u32[]{:S(2)}) copy-start(f32[4,32,128]{2,1,0:T(8,128)} %param.8) | copy-start | bytes 196612
  63.5 18.8 %copy-start.50 = (f32[4,32,128]{2,1,0:T(8,128)S(1)}, f32[4,32,128]{2,1,0:T(8,128)}, u32[]{:S(2)}) copy-start(f32[4,32,128]{2,1,0:T(8,128)} %param.7) | copy-start | bytes 196612
  64.0 24.2 %collective-permute-start.2 = (f32[3,2,128,128]{3,2,1,0:T(8,128)S(1)}, f32[3,2,128,128]{3,2,1,0:T(8,128)S(1)}, u32[]{:S(2)}, u32[]{:S(2)}) collective-permute-start(f32[3,2,128,128]{3,2,1,0:T(8,128)S(1)} %get-tuple-element.67), channel_id=1, source_target_pairs={{0,4},{4,8},{8,12},{12,16},{16,20},{20,24},{24,28},{28,32},{32,36}... | collective-permute-start | bytes 1179656 | tf_op jit(solution)/shard_map/ppermute | solution.py:20
  65.9 22.3 %collective-permute-start.3 = (f32[3,2,128,128]{3,2,1,0:T(8,128)S(1)}, f32[3,2,128,128]{3,2,1,0:T(8,128)S(1)}, u32[]{:S(2)}, u32[]{:S(2)}) collective-permute-start(f32[3,2,128,128]{3,2,1,0:T(8,128)S(1)} %get-tuple-element.68), channel_id=1, source_target_pairs={{4,0},{8,4},{12,8},{16,12},{20,16},{24,20},{28,24},{32,28},{36,32}... | collective-permute-start | bytes 1179656 | tf_op jit(solution)/shard_map/ppermute | solution.py:21
  91.2 47.8 %collective-permute-start.4 = (f32[6,2,128,128]{3,2,1,0:T(8,128)}, f32[6,2,128,128]{3,2,1,0:T(8,128)S(1)}, u32[]{:S(2)}, u32[]{:S(2)}) collective-permute-start(f32[6,2,128,128]{3,2,1,0:T(8,128)} %get-tuple-element.45), channel_id=1, source_target_pairs={{4,0},{8,4},{12,8},{16,12},{20,16},{24,20},{28,24},{32,28},{36,32}... | collective-permute-start | bytes 2359304 | tf_op jit(solution)/shard_map/ppermute | solution.py:21
  93.2 47.6 %collective-permute-start.5 = (f32[6,2,128,128]{3,2,1,0:T(8,128)}, f32[6,2,128,128]{3,2,1,0:T(8,128)S(1)}, u32[]{:S(2)}, u32[]{:S(2)}) collective-permute-start(f32[6,2,128,128]{3,2,1,0:T(8,128)} %get-tuple-element.46), channel_id=1, source_target_pairs={{0,4},{4,8},{8,12},{12,16},{16,20},{20,24},{24,28},{28,32},{32,36}... | collective-permute-start | bytes 2359304 | tf_op jit(solution)/shard_map/ppermute | solution.py:20
  141.3 1.4 copy-start.2
  141.4 1.4 copy-start.6
  141.4 1.4 copy-start.10
  141.4 1.4 copy-start.14
  141.4 1.4 copy-start.18
  144.3 40.2 %copy-start.22 = (f32[4,128,128]{2,1,0:T(8,128)S(1)}, f32[4,128,128]{2,1,0:T(8,128)}, u32[]{:S(2)}) copy-start(f32[4,128,128]{2,1,0:T(8,128)} %copy-done.21) | copy-start | bytes 786436
  144.4 25.8 %collective-permute-start.6 = (f32[3,2,128,128]{3,2,1,0:T(8,128)S(1)}, f32[3,2,128,128]{3,2,1,0:T(8,128)S(1)}, u32[]{:S(2)}, u32[]{:S(2)}) collective-permute-start(f32[3,2,128,128]{3,2,1,0:T(8,128)S(1)} %get-tuple-element.62), channel_id=1, source_target_pairs={{0,4},{4,8},{8,12},{12,16},{16,20},{20,24},{24,28},{28,32},{32,36}... | collective-permute-start | bytes 1179656 | tf_op jit(solution)/shard_map/ppermute | solution.py:20
  155.1 29.5 %collective-permute-start.7 = (f32[3,2,128,128]{3,2,1,0:T(8,128)S(1)}, f32[3,2,128,128]{3,2,1,0:T(8,128)S(1)}, u32[]{:S(2)}, u32[]{:S(2)}) collective-permute-start(f32[3,2,128,128]{3,2,1,0:T(8,128)S(1)} %get-tuple-element.63), channel_id=1, source_target_pairs={{4,0},{8,4},{12,8},{16,12},{20,16},{24,20},{28,24},{32,28},{36,32}... | collective-permute-start | bytes 1179656 | tf_op jit(solution)/shard_map/ppermute | solution.py:21
  186.0 13.4 %copy-start.52 = (s32[1,64,4,4]{1,3,2,0:T(4,128)S(1)}, s32[1,64,4,4]{1,3,2,0:T(4,128)}, u32[]{:S(2)}) copy-start(s32[1,64,4,4]{1,3,2,0:T(4,128)} %get-tuple-element.69) | copy-start | bytes 12292
  186.0 13.4 %copy-start.53 = (s32[1,64,4,4]{1,3,2,0:T(4,128)S(1)}, s32[1,64,4,4]{1,3,2,0:T(4,128)}, u32[]{:S(2)}) copy-start(s32[1,64,4,4]{1,3,2,0:T(4,128)} %get-tuple-element.72) | copy-start | bytes 12292
  187.3 42.7 %collective-permute-start.8 = (f32[6,2,128,128]{3,2,1,0:T(8,128)}, f32[6,2,128,128]{3,2,1,0:T(8,128)S(1)}, u32[]{:S(2)}, u32[]{:S(2)}) collective-permute-start(f32[6,2,128,128]{3,2,1,0:T(8,128)} %get-tuple-element.38), channel_id=1, source_target_pairs={{4,0},{8,4},{12,8},{16,12},{20,16},{24,20},{28,24},{32,28},{36,32}... | collective-permute-start | bytes 2359304 | tf_op jit(solution)/shard_map/ppermute | solution.py:21
  189.2 40.8 %collective-permute-start.9 = (f32[6,2,128,128]{3,2,1,0:T(8,128)}, f32[6,2,128,128]{3,2,1,0:T(8,128)S(1)}, u32[]{:S(2)}, u32[]{:S(2)}) collective-permute-start(f32[6,2,128,128]{3,2,1,0:T(8,128)} %get-tuple-element.39), channel_id=1, source_target_pairs={{0,4},{4,8},{8,12},{12,16},{16,20},{20,24},{24,28},{28,32},{32,36}... | collective-permute-start | bytes 2359304 | tf_op jit(solution)/shard_map/ppermute | solution.py:20
  230.6 1.0 copy-start.3
  230.6 1.1 copy-start.7
  230.6 1.2 copy-start.11
  230.7 1.3 copy-start.15
  230.7 1.3 copy-start.19
  230.7 1.4 copy-start.26
  230.7 1.5 copy-start.29
  230.7 1.5 copy-start.32
  230.7 1.5 copy-start.41
  232.2 1.7 copy-start.39
  233.9 22.6 %copy-start.23 = (f32[4,128,128]{2,1,0:T(8,128)S(1)}, f32[4,128,128]{2,1,0:T(8,128)}, u32[]{:S(2)}) copy-start(f32[4,128,128]{2,1,0:T(8,128)} %copy-done.21) | copy-start | bytes 786436
  234.0 15.7 %collective-permute-start.10 = (f32[3,2,128,128]{3,2,1,0:T(8,128)S(1)}, f32[3,2,128,128]{3,2,1,0:T(8,128)S(1)}, u32[]{:S(2)}, u32[]{:S(2)}) collective-permute-start(f32[3,2,128,128]{3,2,1,0:T(8,128)S(1)} %get-tuple-element.57), channel_id=1, source_target_pairs={{0,4},{4,8},{8,12},{12,16},{16,20},{20,24},{24,28},{28,32},{32,36}... | collective-permute-start | bytes 1179656 | tf_op jit(solution)/shard_map/ppermute | solution.py:20
  240.5 16.0 %collective-permute-start.11 = (f32[3,2,128,128]{3,2,1,0:T(8,128)S(1)}, f32[3,2,128,128]{3,2,1,0:T(8,128)S(1)}, u32[]{:S(2)}, u32[]{:S(2)}) collective-permute-start(f32[3,2,128,128]{3,2,1,0:T(8,128)S(1)} %get-tuple-element.58), channel_id=1, source_target_pairs={{4,0},{8,4},{12,8},{16,12},{20,16},{24,20},{28,24},{32,28},{36,32}... | collective-permute-start | bytes 1179656 | tf_op jit(solution)/shard_map/ppermute | solution.py:21
  259.3 30.1 %collective-permute-start.12 = (f32[6,2,128,128]{3,2,1,0:T(8,128)}, f32[6,2,128,128]{3,2,1,0:T(8,128)S(1)}, u32[]{:S(2)}, u32[]{:S(2)}) collective-permute-start(f32[6,2,128,128]{3,2,1,0:T(8,128)} %get-tuple-element.31), channel_id=1, source_target_pairs={{4,0},{8,4},{12,8},{16,12},{20,16},{24,20},{28,24},{32,28},{36,32}... | collective-permute-start | bytes 2359304 | tf_op jit(solution)/shard_map/ppermute | solution.py:21
  261.2 37.7 %collective-permute-start.13 = (f32[6,2,128,128]{3,2,1,0:T(8,128)}, f32[6,2,128,128]{3,2,1,0:T(8,128)S(1)}, u32[]{:S(2)}, u32[]{:S(2)}) collective-permute-start(f32[6,2,128,128]{3,2,1,0:T(8,128)} %get-tuple-element.32), channel_id=1, source_target_pairs={{0,4},{4,8},{8,12},{12,16},{16,20},{20,24},{24,28},{28,32},{32,36}... | collective-permute-start | bytes 2359304 | tf_op jit(solution)/shard_map/ppermute | solution.py:20
  299.5 1.0 copy-start.4
  299.5 1.0 copy-start.8
  299.5 1.1 copy-start.12
  299.5 1.2 copy-start.16
  299.5 1.2 copy-start.20
  299.5 1.3 copy-start.27
  299.5 1.4 copy-start.30
  299.6 1.4 copy-start.33
  299.6 1.5 copy-start.36
  299.6 1.6 copy-start.38
  299.6 1.7 copy-start.40
  299.6 1.7 copy-start.42
  299.6 1.6 copy-start.46
  303.0 26.8 %copy-start.24 = (f32[4,128,128]{2,1,0:T(8,128)S(1)}, f32[4,128,128]{2,1,0:T(8,128)}, u32[]{:S(2)}) copy-start(f32[4,128,128]{2,1,0:T(8,128)} %copy-done.21) | copy-start | bytes 786436
  303.1 18.5 %collective-permute-start.14 = (f32[3,2,128,128]{3,2,1,0:T(8,128)S(1)}, f32[3,2,128,128]{3,2,1,0:T(8,128)S(1)}, u32[]{:S(2)}, u32[]{:S(2)}) collective-permute-start(f32[3,2,128,128]{3,2,1,0:T(8,128)S(1)} %get-tuple-element.52), channel_id=1, source_target_pairs={{0,4},{4,8},{8,12},{12,16},{16,20},{20,24},{24,28},{28,32},{32,36}... | collective-permute-start | bytes 1179656 | tf_op jit(solution)/shard_map/ppermute | solution.py:20
  313.7 16.1 %collective-permute-start.15 = (f32[3,2,128,128]{3,2,1,0:T(8,128)S(1)}, f32[3,2,128,128]{3,2,1,0:T(8,128)S(1)}, u32[]{:S(2)}, u32[]{:S(2)}) collective-permute-start(f32[3,2,128,128]{3,2,1,0:T(8,128)S(1)} %get-tuple-element.53), channel_id=1, source_target_pairs={{4,0},{8,4},{12,8},{16,12},{20,16},{24,20},{28,24},{32,28},{36,32}... | collective-permute-start | bytes 1179656 | tf_op jit(solution)/shard_map/ppermute | solution.py:21
  (7 other events, 5.0 us)
